TPU v7x, 32 devices: a whole 2x2x4 slice. The times are simulated.
32 devices in a mesh: dp: 8 (over z, y), tensor: 4 (over x, core).
Axes of the slice: x: 2, y: 2, z: 4, core: 2. Of those that a mesh axis runs over, the one named last changes fastest.
Arguments:
- tokens: bfloat16 [16384, 1024], P(('dp', 'tensor')), may hold values from -6 to 6
- output_cotangent: bfloat16 [16384, 1024], P(('dp', 'tensor')), may hold values from -6 to 6
- lengths: int32 [8], P('dp'), may hold values from 1024 to 2048, as said below
- block_place: int32 [8, 32], P('dp'), may hold values from 0 to 31, each once within a row
- random_blocks: int32 [8, 16, 32, 3], P('dp', 'tensor'), may hold values from 0 to 31
- qkv_weight: bfloat16 [1024, 3, 1024], P('dp', None, 'tensor'), may hold values from -0.1875 to 0.1875
- out_weight: bfloat16 [1024, 1024], P('dp', 'tensor'), may hold values from -0.75 to 0.75
- up_weight: bfloat16 [1024, 4096], P('dp', 'tensor'), may hold values from -0.1875 to 0.1875
- down_weight: bfloat16 [1024, 4096], P('dp', 'tensor'), may hold values from -0.09375 to 0.09375
- vectors: float32 [8, 1024], P(None, ('dp', 'tensor')), may hold values from -2 to 2
- hidden_bias: float32 [1, 4096], P(None, ('dp', 'tensor')), may hold values from -3 to 3
Outputs:
- output: bfloat16 [16384, 1024], P(('dp', 'tensor'))
- input_grad: bfloat16 [16384, 1024], P(('dp', 'tensor'))
- qkv_weight_grad: float32 [1024, 3, 1024], P('dp', None, 'tensor')
- out_weight_grad: float32 [1024, 1024], P('dp', 'tensor')
- up_weight_grad: float32 [1024, 4096], P('dp', 'tensor')
- down_weight_grad: float32 [1024, 4096], P('dp', 'tensor')
- vectors_grad: float32 [8, 1024], P(None, ('dp', 'tensor'))
- hidden_bias_grad: float32 [1, 4096], P(None, ('dp', 'tensor'))
Inputs may be any that keep to these rules, and one draw needn't show every extreme that they name: `lengths`: one sequence has exactly 2048 tokens. `block_place`: each row is a permutation.
All inputs are finite; a program needn't handle non-finite values.
Results may differ from a plain program's by a relative error of at most 0.015.
Values may be sent and summed in bfloat16 or wider, within the bound.
No kernel may reach another device: no remote copies, remote signals or barrier semaphores. Data moves between devices by JAX's collectives and lax.ppermute only.
A program may use at most 192 MiB of HBM per device.

v0:
```python
import math
import jax
import jax.numpy as jnp
from jax import lax
from jax.sharding import PartitionSpec as P

HEAD_DIM = 64
BLOCK = 64
EPS = 1e-05
NEGATIVE = -1e30


def in_blocks(value, dim, count):
    before, after = (value.shape[:dim], value.shape[dim + 1 :])
    return jnp.moveaxis(value.reshape(*before, count, -1, *after), dim, 0)


def sent_and_summed(value, axis, dim):
    count = lax.axis_size(axis)
    blocks = lax.all_to_all(in_blocks(value, dim, count), axis, 0, 0, tiled=True)
    return jnp.sum(blocks.astype(jnp.float32), axis=0)


def in_one_piece(arrays, axis, dim, along):
    widths = [math.prod(a.shape[along:]) for a in arrays]
    both = jnp.concatenate(
        [a.reshape(*a.shape[:along], w) for a, w in zip(arrays, widths)], axis=along
    )
    result = sent_and_summed(both, axis, dim)
    blocks = jnp.split(result, [sum(widths[:k]) for k in range(1, len(widths))], axis=along)
    return tuple(
        (b.reshape(*result.shape[:along], *a.shape[along:]) for a, b in zip(arrays, blocks))
    )


def layer_norm_parts(input_rows, gain_row, shift_row):
    centred = input_rows - jnp.mean(input_rows, axis=-1, keepdims=True)
    inverse = lax.rsqrt(jnp.mean(centred * centred, axis=-1, keepdims=True) + EPS)
    unit_rows = centred * inverse
    return (unit_rows * gain_row + shift_row, unit_rows, inverse)


def layer_norm_back(grad_normed, unit_rows, inverse, gain_row):
    grad_unit = grad_normed * gain_row
    grad_rows = inverse * (
        grad_unit
        - jnp.mean(grad_unit, axis=-1, keepdims=True)
        - unit_rows * jnp.mean(grad_unit * unit_rows, axis=-1, keepdims=True)
    )
    return (grad_rows, jnp.sum(grad_normed * unit_rows, axis=0), jnp.sum(grad_normed, axis=0))


def gelu_tanh(pre_active):
    return jax.nn.gelu(pre_active, approximate=True)


def gather_rows(local_rows):
    return lax.all_gather(local_rows, "tensor", axis=0, tiled=True)


def sum_rows(partial_rows):
    return lax.psum_scatter(
        partial_rows.astype(jnp.bfloat16), "tensor", scatter_dimension=0, tiled=True
    ).astype(jnp.float32)


def attention_weights(qkv_weight, out_weight):
    return (
        lax.all_gather(qkv_weight, "dp", axis=0, tiled=True),
        lax.all_gather(out_weight, "dp", axis=0, tiled=True),
    )


def feed_weights(up_weight, down_weight):
    return (
        lax.all_gather(up_weight, "dp", axis=0, tiled=True),
        lax.all_gather(down_weight, "dp", axis=0, tiled=True),
    )


def block_masks(length, placing, chosen):
    nblocks = (length + BLOCK - 1) // BLOCK
    query_seq = placing[:, None]
    key_seq = placing[None, :]
    common = (
        (query_seq == 0)
        | (query_seq == nblocks - 1)
        | (key_seq == 0)
        | (key_seq == nblocks - 1)
        | (jnp.abs(query_seq - key_seq) <= 1)
    )
    by_query = jnp.take(chosen, placing, axis=1)
    random_hit = jnp.any(by_query[:, :, None, :] == key_seq[None, :, :, None], axis=-1)
    allowed = common[None] | random_hit
    positions = placing[:, None] * BLOCK + jnp.arange(BLOCK, dtype=jnp.int32)[None, :]
    return (allowed, positions < length)


def tile_scores(query_tile, key_rows, allowed_tile, key_valid, score_scale):
    scores = (
        jnp.einsum("qhd,khd->hqk", query_tile, key_rows, preferred_element_type=jnp.float32)
        * score_scale
    )
    heads_here = allowed_tile.shape[0]
    blocks_here = allowed_tile.shape[1]
    block_size = key_valid.shape[1]
    scores = scores.reshape(heads_here, blocks_here, block_size, key_valid.shape[0], block_size)
    keep_mask = allowed_tile[:, :, None, :, None] & key_valid[None, None, None, :, :]
    scores = jnp.where(keep_mask, scores, NEGATIVE)
    return scores.reshape(heads_here, blocks_here * block_size, -1)


def project_heads(normed_all, qkv_full, bias_query, bias_value):
    projected = jnp.einsum("td,dcf->ctf", normed_all, qkv_full, preferred_element_type=jnp.float32)
    head_shape = (normed_all.shape[0], -1, HEAD_DIM)
    queries = (projected[0] + bias_query).astype(jnp.bfloat16).reshape(head_shape)
    key_rows = projected[1].astype(jnp.bfloat16).reshape(head_shape)
    value_rows = (projected[2] + bias_value).astype(jnp.bfloat16).reshape(head_shape)
    return (queries, key_rows, value_rows)


def attend(queries, key_rows, value_rows, allowed, key_valid, tile_rows, score_scale):
    per_tile = tile_rows // BLOCK

    def one_tile(number):
        query_tile = lax.dynamic_slice_in_dim(queries, number * tile_rows, tile_rows, 0)
        allowed_tile = lax.dynamic_slice_in_dim(allowed, number * per_tile, per_tile, 1)
        scores = tile_scores(query_tile, key_rows, allowed_tile, key_valid, score_scale)
        row_top = jnp.max(scores, axis=-1, keepdims=True)
        weights = jnp.exp(scores - row_top)
        row_total = jnp.sum(weights, axis=-1, keepdims=True)
        probabilities = (weights / row_total).astype(jnp.bfloat16)
        context_tile = jnp.einsum(
            "hqk,khd->qhd", probabilities, value_rows, preferred_element_type=jnp.float32
        )
        return (
            context_tile.reshape(tile_rows, -1).astype(jnp.bfloat16),
            (row_top + jnp.log(row_total))[..., 0],
        )

    context_tiles, log_totals = lax.map(
        one_tile, jnp.arange(queries.shape[0] // tile_rows, dtype=jnp.int32)
    )
    return (context_tiles.reshape(queries.shape[0], -1), log_totals)


def attend_back(
    queries,
    key_rows,
    value_rows,
    grad_context,
    log_totals,
    allowed,
    key_valid,
    tile_rows,
    score_scale,
):
    per_tile = tile_rows // BLOCK

    def one_tile(state_pair, number):
        grad_keys, grad_values = state_pair
        query_tile = lax.dynamic_slice_in_dim(queries, number * tile_rows, tile_rows, 0)
        grad_tile = lax.dynamic_slice_in_dim(grad_context, number * tile_rows, tile_rows, 0)
        allowed_tile = lax.dynamic_slice_in_dim(allowed, number * per_tile, per_tile, 1)
        scores = tile_scores(query_tile, key_rows, allowed_tile, key_valid, score_scale)
        probabilities = jnp.exp(scores - log_totals[number][:, :, None])
        probs_low = probabilities.astype(jnp.bfloat16)
        grad_probs = jnp.einsum(
            "qhd,khd->hqk", grad_tile, value_rows, preferred_element_type=jnp.float32
        )
        row_inner = jnp.sum(probabilities * grad_probs, axis=-1, keepdims=True)
        grad_scores = (probabilities * (grad_probs - row_inner)).astype(jnp.bfloat16)
        grad_query = (
            jnp.einsum("hqk,khd->qhd", grad_scores, key_rows, preferred_element_type=jnp.float32)
            * score_scale
        )
        grad_keys = (
            grad_keys
            + jnp.einsum(
                "hqk,qhd->khd", grad_scores, query_tile, preferred_element_type=jnp.float32
            )
            * score_scale
        )
        grad_values = grad_values + jnp.einsum(
            "hqk,qhd->khd", probs_low, grad_tile, preferred_element_type=jnp.float32
        )
        return ((grad_keys, grad_values), grad_query.astype(jnp.bfloat16))

    zero_state = jnp.zeros(key_rows.shape, jnp.float32)
    final_state, grad_queries = lax.scan(
        one_tile,
        (zero_state, zero_state),
        jnp.arange(queries.shape[0] // tile_rows, dtype=jnp.int32),
    )
    flat_queries = grad_queries.reshape(queries.shape[0], -1)
    flat_keys = final_state[0].reshape(flat_queries.shape).astype(jnp.bfloat16)
    flat_values = final_state[1].reshape(flat_queries.shape).astype(jnp.bfloat16)
    return (flat_queries, flat_keys, flat_values)


def per_device(
    tokens,
    output_cotangent,
    lengths,
    block_place,
    random_blocks,
    qkv_weight,
    out_weight,
    up_weight,
    down_weight,
    vectors,
    hidden_bias,
):
    vectors_full, hidden_full = (
        lax.all_gather(vectors, ("dp", "tensor"), axis=1, tiled=True),
        lax.all_gather(hidden_bias, ("dp", "tensor"), axis=1, tiled=True),
    )
    width_local = qkv_weight.shape[2]
    units_local = up_weight.shape[1]
    position = lax.axis_index("tensor")
    head_start = position * width_local
    unit_start = position * units_local
    bias_query = lax.dynamic_slice_in_dim(vectors_full[6], head_start, width_local)
    bias_value = lax.dynamic_slice_in_dim(vectors_full[7], head_start, width_local)
    bias_hidden = lax.dynamic_slice_in_dim(hidden_full[0], unit_start, units_local)
    allowed, key_valid = block_masks(lengths[0], block_place[0], random_blocks[0])
    slot_rows = tokens.shape[0] * lax.axis_size("tensor")
    tile_rows = min(512, slot_rows)
    score_scale = HEAD_DIM ** (-0.5)
    residual_in = tokens.astype(jnp.float32)
    qkv_full, out_full = attention_weights(qkv_weight, out_weight)
    normed_one, unit_one, inverse_one = layer_norm_parts(
        residual_in, vectors_full[0], vectors_full[1]
    )
    normed_one_all = gather_rows(normed_one.astype(jnp.bfloat16))
    queries, key_rows, value_rows = project_heads(normed_one_all, qkv_full, bias_query, bias_value)
    context, log_totals = attend(
        queries, key_rows, value_rows, allowed, key_valid, tile_rows, score_scale
    )
    attended = sum_rows(
        jnp.einsum("tf,df->td", context, out_full, preferred_element_type=jnp.float32)
    )
    middle = residual_in + attended + vectors_full[4]
    normed_two, unit_two, inverse_two = layer_norm_parts(middle, vectors_full[2], vectors_full[3])
    up_full, down_full = feed_weights(up_weight, down_weight)
    normed_two_all = gather_rows(normed_two.astype(jnp.bfloat16))
    hidden = jnp.dot(normed_two_all, up_full, preferred_element_type=jnp.float32) + bias_hidden
    active = gelu_tanh(hidden).astype(jnp.bfloat16)
    feed_out = sum_rows(
        jnp.einsum("tf,df->td", active, down_full, preferred_element_type=jnp.float32)
    )
    output = (middle + feed_out + vectors_full[5]).astype(jnp.bfloat16)
    grad_all = gather_rows(output_cotangent)
    up_back, down_back = feed_weights(up_weight, down_weight)
    normed_two_back = gather_rows(normed_two.astype(jnp.bfloat16))
    hidden_back = (
        jnp.dot(normed_two_back, up_back, preferred_element_type=jnp.float32) + bias_hidden
    )
    active_back = gelu_tanh(hidden_back).astype(jnp.bfloat16)
    grad_active = jnp.dot(grad_all, down_back, preferred_element_type=jnp.float32)
    gelu_pullback = jax.vjp(gelu_tanh, hidden_back)[1]
    grad_hidden = gelu_pullback(grad_active)[0].astype(jnp.bfloat16)
    grad_up = jnp.einsum(
        "td,tf->df", normed_two_back, grad_hidden, preferred_element_type=jnp.float32
    )
    grad_down = jnp.einsum("td,tf->df", grad_all, active_back, preferred_element_type=jnp.float32)
    grad_bias_hidden = jnp.sum(grad_hidden, axis=0, dtype=jnp.float32)
    grad_normed_two = sum_rows(
        jnp.einsum("tf,df->td", grad_hidden, up_back, preferred_element_type=jnp.float32)
    )
    up_weight_grad, down_weight_grad = (
        lax.psum_scatter(grad_up, "dp", scatter_dimension=0, tiled=True),
        lax.psum_scatter(grad_down, "dp", scatter_dimension=0, tiled=True),
    )
    cotangent_rows = output_cotangent.astype(jnp.float32)
    grad_middle_part, grad_gain_two, grad_shift_two = layer_norm_back(
        grad_normed_two, unit_two, inverse_two, vectors_full[2]
    )
    grad_middle = cotangent_rows + grad_middle_part
    grad_attended_all = gather_rows(grad_middle.astype(jnp.bfloat16))
    qkv_back, out_back = attention_weights(qkv_weight, out_weight)
    normed_one_back = gather_rows(normed_one.astype(jnp.bfloat16))
    queries_back, keys_back, values_back = project_heads(
        normed_one_back, qkv_back, bias_query, bias_value
    )
    grad_context = jnp.dot(grad_attended_all, out_back, preferred_element_type=jnp.float32).astype(
        jnp.bfloat16
    )
    grad_out_weight = jnp.einsum(
        "td,tf->df", grad_attended_all, context, preferred_element_type=jnp.float32
    )
    grad_context_heads = grad_context.reshape(slot_rows, -1, HEAD_DIM)
    grad_queries, grad_keys, grad_values = attend_back(
        queries_back,
        keys_back,
        values_back,
        grad_context_heads,
        log_totals,
        allowed,
        key_valid,
        tile_rows,
        score_scale,
    )
    grad_projected = jnp.stack([grad_queries, grad_keys, grad_values])
    grad_qkv = jnp.einsum(
        "td,ctf->dcf", normed_one_back, grad_projected, preferred_element_type=jnp.float32
    )
    grad_normed_one = sum_rows(
        jnp.einsum("ctf,dcf->td", grad_projected, qkv_back, preferred_element_type=jnp.float32)
    )
    qkv_weight_grad, out_weight_grad = in_one_piece(
        (grad_qkv.astype(jnp.bfloat16), grad_out_weight.astype(jnp.bfloat16)), "dp", 0, 1
    )
    grad_input_part, grad_gain_one, grad_shift_one = layer_norm_back(
        grad_normed_one, unit_one, inverse_one, vectors_full[0]
    )
    input_grad = (grad_middle + grad_input_part).astype(jnp.bfloat16)
    local_grads = jnp.stack(
        [
            grad_gain_one,
            grad_shift_one,
            grad_gain_two,
            grad_shift_two,
            jnp.sum(grad_middle, axis=0),
            jnp.sum(cotangent_rows, axis=0),
        ]
    )
    head_bias_grads = jnp.stack(
        [
            jnp.sum(grad_queries, axis=0, dtype=jnp.float32),
            jnp.sum(grad_values, axis=0, dtype=jnp.float32),
        ]
    )
    head_grads = lax.dynamic_update_slice(
        jnp.zeros((2, vectors_full.shape[1]), jnp.float32), head_bias_grads, (0, head_start)
    )
    hidden_grads = lax.dynamic_update_slice(
        jnp.zeros(hidden_full.shape, jnp.float32), grad_bias_hidden[None, :], (0, unit_start)
    )
    vectors_grad, hidden_bias_grad = (
        lax.psum_scatter(
            jnp.concatenate([local_grads, head_grads], axis=0),
            ("dp", "tensor"),
            scatter_dimension=1,
            tiled=True,
        ),
        lax.psum_scatter(hidden_grads, ("dp", "tensor"), scatter_dimension=1, tiled=True),
    )
    return (
        output,
        input_grad,
        qkv_weight_grad,
        out_weight_grad,
        up_weight_grad,
        down_weight_grad,
        vectors_grad,
        hidden_bias_grad,
    )


def solution(mesh):
    placed = (
        P(("dp", "tensor"), None),
        P(("dp", "tensor"), None),
        P("dp"),
        P("dp", None),
        P("dp", "tensor", None, None),
        P("dp", None, "tensor"),
        P("dp", "tensor"),
        P("dp", "tensor"),
        P("dp", "tensor"),
        P(None, ("dp", "tensor")),
        P(None, ("dp", "tensor")),
    )
    return jax.shard_map(
        per_device,
        mesh=mesh,
        in_specs=placed,
        out_specs=(
            P(("dp", "tensor"), None),
            P(("dp", "tensor"), None),
            P("dp", None, "tensor"),
            P("dp", "tensor"),
            P("dp", "tensor"),
            P("dp", "tensor"),
            P(None, ("dp", "tensor")),
            P(None, ("dp", "tensor")),
        ),
        check_vma=False,
    )
```

profile of v0, /device:TPU:0, one launch (start us, length us, event | category | flops | bytes accessed | tf_op | source)
XLA Modules:
  0.0 1534.6 jit_solution(7175553528561986382)
XLA Ops:
  9.1 44.2 %all-gather = f32[32,32,8]{1,2,0:T(8,128)S(1)} all-gather(f32[1,32,8]{1,2,0:T(8,128)} %bitcast.196), channel_id=1, replica_groups=mesh['dp'=8,'tensor'=4] {'dp','tensor'}, dimensions={0}, use_global_device_ids=true | all-gather | bytes 33792 | tf_op jit(solution)/shard_map/all_gather | solution.py:215
  62.7 33.9 %all_gather.39 = bf16[1024,256]{1,0:T(8,128)(2,1)} all-gather(bf16[128,256]{1,0:T(8,128)(2,1)S(1)} %copy-done.18), channel_id=1, replica_groups=mesh['dp'=8,'tensor'=4] {'dp'}, dimensions={0}, use_global_device_ids=true | all-gather | bytes 589824 | tf_op jit(solution)/shard_map/all_gather | solution.py:70
  104.3 192.3 %while.28 = (s32[]{:T(128)}, bf16[4,512,256]{2,1,0:T(8,128)(2,1)}, f32[4,4,512]{2,1,0:T(4,128)S(1)}, s32[4]{0:T(128)S(1)}, pred[4,32,32]{2,1,0:T(8,128)(4,1)S(1)...) while((s32[]{:T(128)}, bf16[4,512,256]{2,1,0:T(8,128)(2,1)}, ...), condition=%wide.region_6.7_spmd.clone, body=%wide.region_3.6_spmd.clone.sunk | while | flops 1124272128 | bytes 96148904 | solution.py:141
  112.5 22.8 %broadcast_in_dim.121 = pred[4,512,2048]{2,1,0:T(32,128)(4,1)} reshape(pred[4,8,64,32,64]{4,3,2,1,0:T(32,128)(4,1)} %broadcast_in_dim.120) | data formatting | bytes 8388608 | tf_op jit(solution)/shard_map/while/body/eval_jaxpr/jit(_where)/broadcast_in_dim | solution.py:109
  145.6 5.8 fusion.136
  160.5 22.8 %broadcast_in_dim.121 = pred[4,512,2048]{2,1,0:T(32,128)(4,1)} reshape(pred[4,8,64,32,64]{4,3,2,1,0:T(32,128)(4,1)} %broadcast_in_dim.120) | data formatting | bytes 8388608 | tf_op jit(solution)/shard_map/while/body/eval_jaxpr/jit(_where)/broadcast_in_dim | solution.py:109
  193.7 5.8 fusion.136
  208.6 22.8 %broadcast_in_dim.121 = pred[4,512,2048]{2,1,0:T(32,128)(4,1)} reshape(pred[4,8,64,32,64]{4,3,2,1,0:T(32,128)(4,1)} %broadcast_in_dim.120) | data formatting | bytes 8388608 | tf_op jit(solution)/shard_map/while/body/eval_jaxpr/jit(_where)/broadcast_in_dim | solution.py:109
  256.7 22.8 %broadcast_in_dim.121 = pred[4,512,2048]{2,1,0:T(32,128)(4,1)} reshape(pred[4,8,64,32,64]{4,3,2,1,0:T(32,128)(4,1)} %broadcast_in_dim.120) | data formatting | bytes 8388608 | tf_op jit(solution)/shard_map/while/body/eval_jaxpr/jit(_where)/broadcast_in_dim | solution.py:109
  289.9 5.8 fusion.136
  301.9 41.5 %reduce-scatter.13.cloned.1.call-done = bf16[512,1024]{1,0:T(8,128)(2,1)} async-done(((bf16[2048,1024]{1,0:T(8,128)(2,1)}), bf16[512,1024]{1,0:T(8,128)(2,1)}) %reduce-scatter.13.cloned.1.call-update) | async-done | bytes 1048592 | tf_op jit(solution)/shard_map/reduce_scatter | solution.py:62
  349.9 40.5 %all_gather.42 = f32[1,4096]{1,0:T(1,128)S(1)} all-gather(f32[1,128]{1,0:T(1,128)S(1)} %copy-done.36), channel_id=1, replica_groups=mesh['dp'=8,'tensor'=4] {'dp','tensor'}, dimensions={1}, use_global_device_ids=true | all-gather | bytes 16896 | tf_op jit(solution)/shard_map/all_gather | solution.py:216
  394.9 35.1 %all-gather.13.cloned.1.call-done = bf16[2048,1024]{1,0:T(8,128)(2,1)} async-done(((bf16[512,1024]{1,0:T(8,128)(2,1)}), bf16[2048,1024]{1,0:T(8,128)(2,1)}) %all-gather.13.cloned.1.call-update) | async-done | bytes 4194320 | tf_op jit(solution)/shard_map/all_gather | solution.py:58
  430.0 10.6 fusion.87
  440.6 40.9 %all-gather.17.cloned.1.call-done = bf16[1024,1024]{1,0:T(8,128)(2,1)} async-done(((bf16[128,1024]{1,0:T(8,128)(2,1)}), bf16[1024,1024]{1,0:T(8,128)(2,1)}) %all-gather.17.cloned.1.call-update) | async-done | bytes 2097168 | tf_op jit(solution)/shard_map/all_gather | solution.py:77
  481.5 34.6 %all-gather.19.cloned.1.call-done = bf16[2048,1024]{1,0:T(8,128)(2,1)} async-done(((bf16[512,1024]{1,0:T(8,128)(2,1)}), bf16[2048,1024]{1,0:T(8,128)(2,1)}) %all-gather.19.cloned.1.call-update) | async-done | bytes 4194320 | tf_op jit(solution)/shard_map/all_gather | solution.py:58
  516.1 14.3 convert_reduce_fusion
  532.5 6.4 convolution_convert_fusion.1
  539.1 11.7 convolution_convert_fusion.2
  550.9 32.6 %reduce-scatter.17.cloned.1.call-done = bf16[512,1024]{1,0:T(8,128)(2,1)} async-done(((bf16[2048,1024]{1,0:T(8,128)(2,1)}), bf16[512,1024]{1,0:T(8,128)(2,1)}) %reduce-scatter.17.cloned.1.call-update) | async-done | bytes 1048592 | tf_op jit(solution)/shard_map/reduce_scatter | solution.py:62
  586.8 43.7 %reduce-scatter.15.cloned.1.call-done = bf16[512,1024]{1,0:T(8,128)(2,1)} async-done(((bf16[2048,1024]{1,0:T(8,128)(2,1)}), bf16[512,1024]{1,0:T(8,128)(2,1)}) %reduce-scatter.15.cloned.1.call-update) | async-done | bytes 1048592 | tf_op jit(solution)/shard_map/reduce_scatter | solution.py:62
  637.6 34.6 %all-gather.21.cloned.1.call-done = bf16[2048,1024]{1,0:T(8,128)(2,1)} async-done(((bf16[512,1024]{1,0:T(8,128)(2,1)}), bf16[2048,1024]{1,0:T(8,128)(2,1)}) %all-gather.21.cloned.1.call-update) | async-done | bytes 4194320 | tf_op jit(solution)/shard_map/all_gather | solution.py:58
  676.7 328.6 %while.29 = (s32[]{:T(128)}, f32[2048,4,64]{0,2,1:T(8,128)}, f32[2048,4,64]{0,2,1:T(8,128)}, bf16[4,512,4,64]{1,3,2,0:T(8,128)(2,1)}, s32[4]{0:T(128)S(1)}, /*in...) while((s32[]{:T(128)}, f32[2048,4,64]{0,2,1:T(8,128)}, ...), condition=%wide.region_16.17_spmd.clone, body=%wide.region_14.16_spmd.clone.sunk | while | flops 2725054464 | bytes 256294480 | solution.py:190
  687.1 22.8 %broadcast_in_dim.123 = pred[4,512,2048]{2,1,0:T(32,128)(4,1)} reshape(pred[4,8,64,32,64]{4,3,2,1,0:T(32,128)(4,1)} %broadcast_in_dim.122) | data formatting | bytes 8388608 | tf_op jit(solution)/shard_map/while/body/eval_jaxpr/jit(_where)/broadcast_in_dim | solution.py:109
  709.9 9.2 fusion.146
  719.1 12.7 multiply_reduce_fusion.3
  731.8 11.5 multiply_convert_fusion.5
  768.5 22.8 %broadcast_in_dim.123 = pred[4,512,2048]{2,1,0:T(32,128)(4,1)} reshape(pred[4,8,64,32,64]{4,3,2,1,0:T(32,128)(4,1)} %broadcast_in_dim.122) | data formatting | bytes 8388608 | tf_op jit(solution)/shard_map/while/body/eval_jaxpr/jit(_where)/broadcast_in_dim | solution.py:109
  791.4 9.2 fusion.146
  800.6 12.7 multiply_reduce_fusion.3
  813.3 11.5 multiply_convert_fusion.5
  850.8 22.8 %broadcast_in_dim.123 = pred[4,512,2048]{2,1,0:T(32,128)(4,1)} reshape(pred[4,8,64,32,64]{4,3,2,1,0:T(32,128)(4,1)} %broadcast_in_dim.122) | data formatting | bytes 8388608 | tf_op jit(solution)/shard_map/while/body/eval_jaxpr/jit(_where)/broadcast_in_dim | solution.py:109
  873.6 9.2 fusion.146
  882.8 12.7 multiply_reduce_fusion.3
  895.5 11.5 multiply_convert_fusion.5
  933.0 22.8 %broadcast_in_dim.123 = pred[4,512,2048]{2,1,0:T(32,128)(4,1)} reshape(pred[4,8,64,32,64]{4,3,2,1,0:T(32,128)(4,1)} %broadcast_in_dim.122) | data formatting | bytes 8388608 | tf_op jit(solution)/shard_map/while/body/eval_jaxpr/jit(_where)/broadcast_in_dim | solution.py:109
  955.8 9.2 fusion.146
  965.0 12.7 multiply_reduce_fusion.3
  977.7 11.5 multiply_convert_fusion.5
  1020.0 7.8 bitcast_convert_fusion
  1030.6 13.3 convolution_bitcast_fusion
  1044.7 27.9 %reduce-scatter.19.cloned.1.call-done = bf16[512,1024]{1,0:T(8,128)(2,1)} async-done(((bf16[2048,1024]{1,0:T(8,128)(2,1)}), bf16[512,1024]{1,0:T(8,128)(2,1)}) %reduce-scatter.19.cloned.1.call-update) | async-done | bytes 1048592 | tf_op jit(solution)/shard_map/reduce_scatter | solution.py:62
  1076.5 10.0 fusion.88
  1091.6 7.8 fusion.73
  1109.1 105.7 %reduce-scatter.27.cloned.1.call-done = f32[128,1]{1,0:T(8,128)} async-done(((f32[4096,1]{1,0:T(8,128)}), f32[128,1]{1,0:T(8,128)}) %reduce-scatter.27.cloned.1.call-update) | async-done | bytes 528
  1216.2 87.6 %reduce-scatter.23.cloned.1.call-done = f32[128,1024]{0,1:T(8,128)} async-done(((f32[1024,1024]{0,1:T(8,128)}), f32[128,1024]{0,1:T(8,128)}) %reduce-scatter.23.cloned.1.call-update) | async-done | bytes 524304 | tf_op jit(solution)/shard_map/reduce_scatter | solution.py:273
  1314.7 124.8 %reduce-scatter.25.cloned.1.call-done = f32[32,8]{1,0:T(8,128)} async-done(((f32[1024,8]{1,0:T(8,128)}), f32[32,8]{1,0:T(8,128)}) %reduce-scatter.25.cloned.1.call-update) | async-done | bytes 1040
  1440.9 86.9 %reduce-scatter.21.cloned.1.call-done = f32[128,1024]{1,0:T(8,128)} async-done(((f32[1024,1024]{1,0:T(8,128)}), f32[128,1024]{1,0:T(8,128)}) %reduce-scatter.21.cloned.1.call-update) | async-done | bytes 524304 | tf_op jit(solution)/shard_map/reduce_scatter | solution.py:272
  (303 shorter events, 270.8 us)
Async XLA Ops:
  7.2 54.0 %copy-start.32 = (s32[1,4,32,3]{2,1,3,0:T(4,128)S(1)}, s32[1,4,32,3]{2,1,3,0:T(4,128)}, u32[]{:S(2)}) copy-start(s32[1,4,32,3]{2,1,3,0:T(4,128)} %param.19) | copy-start | bytes 4612
  7.2 54.2 %copy-start.31 = (s32[1,32]{1,0:T(1,128)S(1)}, s32[1,32]{1,0:T(1,128)}, u32[]{:S(2)}) copy-start(s32[1,32]{1,0:T(1,128)} %param.18) | copy-start | bytes 388
  7.2 55.5 %copy-start.18 = (bf16[128,256]{1,0:T(8,128)(2,1)S(1)}, bf16[128,256]{1,0:T(8,128)(2,1)}, u32[]{:S(2)}) copy-start(bf16[128,256]{1,0:T(8,128)(2,1)} %param.21) | copy-start | bytes 196612
  7.2 89.3 %all-gather.11.cloned.1.call-start = ((), (), s32[]{:S(2)}) async-start(), calls=%async_computation.10 | async-start | bytes 1769472 | tf_op jit(solution)/shard_map/all_gather | solution.py:69
  9.0 87.5 %all-gather.9.cloned.1.call-start = ((), (), s32[]{:S(2)}) async-start(), calls=%async_computation.9 | async-start | bytes 5242880 | tf_op jit(solution)/shard_map/all_gather | solution.py:58
  60.4 282.9 %reduce-scatter.13.cloned.1.call-start = ((), (), s32[]{:S(2)}) async-start(), calls=%async_computation.11 | async-start | bytes 5242880 | tf_op jit(solution)/shard_map/reduce_scatter | solution.py:62
  104.3 192.3 %copy-start.13 = (bf16[1024,256]{1,0:T(8,128)(2,1)S(1)}, bf16[1024,256]{1,0:T(8,128)(2,1)}, u32[]{:S(2)}) copy-start(bf16[1024,256]{1,0:T(8,128)(2,1)} %all_gather.39) | copy-start | bytes 1572868
  183.4 5.6 copy-start.1
  301.0 42.3 %copy-start.3 = (bf16[512,1024]{1,0:T(8,128)(2,1)S(1)}, bf16[512,1024]{1,0:T(8,128)(2,1)}, u32[]{:S(2)}) copy-start(bf16[512,1024]{1,0:T(8,128)(2,1)} %param.15) | copy-start | bytes 3145732
  301.0 42.3 %copy-start.16 = (f32[1,1024]{1,0:T(1,128)S(1)}, f32[1,1024]{1,0:T(1,128)}, u32[]{:S(2)}) copy-start(f32[1,1024]{1,0:T(1,128)} %get-tuple-element.298) | copy-start | bytes 12292
  301.0 45.9 %copy-start.17 = (f32[1,1024]{1,0:T(1,128)S(1)}, f32[1,1024]{1,0:T(1,128)}, u32[]{:S(2)}) copy-start(f32[1,1024]{1,0:T(1,128)} %get-tuple-element.297) | copy-start | bytes 12292
  301.1 45.9 %copy-start.26 = (f32[1,1024]{1,0:T(1,128)S(1)}, f32[1,1024]{1,0:T(1,128)}, u32[]{:S(2)}) copy-start(f32[1,1024]{1,0:T(1,128)} %get-tuple-element.296) | copy-start | bytes 12292
  301.1 93.8 %all-gather.15.cloned.1.call-start = ((), (), s32[]{:S(2)}) async-start(), calls=%async_computation.13 | async-start | bytes 2359296 | tf_op jit(solution)/shard_map/all_gather | solution.py:76
  301.7 128.3 %all-gather.13.cloned.1.call-start = ((), (), s32[]{:S(2)}) async-start(), calls=%async_computation.12 | async-start | bytes 5242880 | tf_op jit(solution)/shard_map/all_gather | solution.py:58
  348.5 133.0 %all-gather.17.cloned.1.call-start = ((), (), s32[]{:S(2)}) async-start(), calls=%async_computation.14 | async-start | bytes 2359296 | tf_op jit(solution)/shard_map/all_gather | solution.py:77
  349.1 167.0 %all-gather.19.cloned.1.call-start = ((), (), s32[]{:S(2)}) async-start(), calls=%async_computation.16 | async-start | bytes 5242880 | tf_op jit(solution)/shard_map/all_gather | solution.py:58
  349.9 233.6 %reduce-scatter.17.cloned.1.call-start = ((), (), s32[]{:S(2)}) async-start(), calls=%async_computation.17 | async-start | bytes 5242880 | tf_op jit(solution)/shard_map/reduce_scatter | solution.py:62
  390.4 148.7 %copy-start.33 = (f32[1,1024]{1,0:T(1,128)}, f32[1,1024]{1,0:T(1,128)S(1)}, u32[]{:S(2)}) copy-start(f32[1,1024]{1,0:T(1,128)S(1)} %constant_dynamic-slice_fusion.2) | copy-start | bytes 12292
  516.1 16.3 %copy-start.37 = (bf16[1024,1024]{1,0:T(8,128)(2,1)S(1)}, bf16[1024,1024]{1,0:T(8,128)(2,1)}, u32[]{:S(2)}) copy-start(bf16[1024,1024]{1,0:T(8,128)(2,1)} %all-gather.15.cloned.1.call-done) | copy-start | bytes 6291460
  538.8 91.7 %reduce-scatter.15.cloned.1.call-start = ((), (), s32[]{:S(2)}) async-start(), calls=%async_computation.15 | async-start | bytes 5242880 | tf_op jit(solution)/shard_map/reduce_scatter | solution.py:62
  550.8 79.7 %copy-start.25 = (f32[1,1024]{1,0:T(1,128)S(1)}, f32[1,1024]{1,0:T(1,128)}, u32[]{:S(2)}) copy-start(f32[1,1024]{1,0:T(1,128)} %get-tuple-element.295) | copy-start | bytes 12292
  550.9 121.3 %all-gather.21.cloned.1.call-start = ((), (), s32[]{:S(2)}) async-start(), calls=%async_computation.18 | async-start | bytes 5242880 | tf_op jit(solution)/shard_map/all_gather | solution.py:58
  635.1 37.1 %copy-start.14 = (bf16[1024,256]{1,0:T(8,128)(2,1)S(1)}, bf16[1024,256]{1,0:T(8,128)(2,1)}, u32[]{:S(2)}) copy-start(bf16[1024,256]{1,0:T(8,128)(2,1)} %all_gather.39) | copy-start | bytes 1572868
  637.6 435.0 %reduce-scatter.19.cloned.1.call-start = ((), (), s32[]{:S(2)}) async-start(), calls=%async_computation.19 | async-start | bytes 5242880 | tf_op jit(solution)/shard_map/reduce_scatter | solution.py:62
  709.9 9.2 copy-start.2
  731.8 15.4 %copy-start = (f32[4,512,2048]{2,1,0:T(8,128)S(1)}, f32[4,512,2048]{2,1,0:T(8,128)}, u32[]{:S(2)}) copy-start(f32[4,512,2048]{2,1,0:T(8,128)} %get-tuple-element.455) | copy-start | bytes 50331652 | tf_op jit(solution)/shard_map/while
  791.4 9.2 copy-start.2
  813.3 15.4 %copy-start = (f32[4,512,2048]{2,1,0:T(8,128)S(1)}, f32[4,512,2048]{2,1,0:T(8,128)}, u32[]{:S(2)}) copy-start(f32[4,512,2048]{2,1,0:T(8,128)} %get-tuple-element.455) | copy-start | bytes 50331652 | tf_op jit(solution)/shard_map/while
  873.6 9.2 copy-start.2
  895.5 15.4 %copy-start = (f32[4,512,2048]{2,1,0:T(8,128)S(1)}, f32[4,512,2048]{2,1,0:T(8,128)}, u32[]{:S(2)}) copy-start(f32[4,512,2048]{2,1,0:T(8,128)} %get-tuple-element.455) | copy-start | bytes 50331652 | tf_op jit(solution)/shard_map/while
  955.8 9.2 copy-start.2
  977.7 15.4 %copy-start = (f32[4,512,2048]{2,1,0:T(8,128)S(1)}, f32[4,512,2048]{2,1,0:T(8,128)}, u32[]{:S(2)}) copy-start(f32[4,512,2048]{2,1,0:T(8,128)} %get-tuple-element.455) | copy-start | bytes 50331652 | tf_op jit(solution)/shard_map/while
  1008.1 9.3 copy-start.7
  1020.0 7.8 copy-start.15
  1027.9 186.9 %reduce-scatter.27.cloned.1.call-start = ((), (), s32[]{:S(2)}) async-start(), calls=%async_computation.23 | async-start | bytes 2162688
  1030.6 273.2 %reduce-scatter.23.cloned.1.call-start = ((), (), s32[]{:S(2)}) async-start(), calls=%async_computation.21 | async-start | bytes 4718592 | tf_op jit(solution)/shard_map/reduce_scatter | solution.py:273
  1043.9 28.6 %copy-start.4 = (bf16[512,1024]{1,0:T(8,128)(2,1)S(1)}, bf16[512,1024]{1,0:T(8,128)(2,1)}, u32[]{:S(2)}) copy-start(bf16[512,1024]{1,0:T(8,128)(2,1)} %param.15) | copy-start | bytes 3145732
  1043.9 28.6 %copy-start.20 = (f32[1,1024]{1,0:T(1,128)S(1)}, f32[1,1024]{1,0:T(1,128)}, u32[]{:S(2)}) copy-start(f32[1,1024]{1,0:T(1,128)} %copy-done.19) | copy-start | bytes 12292
  1043.9 28.6 %copy-start.22 = (f32[512]{0:T(512)S(1)}, f32[512]{0:T(512)}, u32[]{:S(2)}) copy-start(f32[512]{0:T(512)} %copy-done.21) | copy-start | bytes 6148
  1043.9 28.6 %copy-start.24 = (f32[512]{0:T(512)S(1)}, f32[512]{0:T(512)}, u32[]{:S(2)}) copy-start(f32[512]{0:T(512)} %copy-done.23) | copy-start | bytes 6148
  1044.0 31.4 %copy-start.27 = (f32[1024]{0:T(1024)S(1)}, f32[1024]{0:T(1024)}, u32[]{:S(2)}) copy-start(f32[1024]{0:T(1024)} %get-tuple-element.227) | copy-start | bytes 12292
  1044.0 31.4 %copy-start.28 = (f32[1024]{0:T(1024)S(1)}, f32[1024]{0:T(1024)}, u32[]{:S(2)}) copy-start(f32[1024]{0:T(1024)} %get-tuple-element.233) | copy-start | bytes 12292
  1044.0 31.4 %copy-start.29 = (f32[1024]{0:T(1024)S(1)}, f32[1024]{0:T(1024)}, u32[]{:S(2)}) copy-start(f32[1024]{0:T(1024)} %get-tuple-element.285) | copy-start | bytes 12292
  1044.0 31.4 %copy-start.30 = (f32[1024]{0:T(1024)S(1)}, f32[1024]{0:T(1024)}, u32[]{:S(2)}) copy-start(f32[1024]{0:T(1024)} %get-tuple-element.294) | copy-start | bytes 12292
  1044.0 395.5 %reduce-scatter.25.cloned.1.call-start = ((), (), s32[]{:S(2)}) async-start(), calls=%async_computation.22 | async-start | bytes 540672
  1076.5 451.3 %reduce-scatter.21.cloned.1.call-start = ((), (), s32[]{:S(2)}) async-start(), calls=%async_computation.20 | async-start | bytes 4718592 | tf_op jit(solution)/shard_map/reduce_scatter | solution.py:272
  1103.4 208.3 %copy-start.10 = (f32[512,1024]{1,0:T(8,128)S(1)}, f32[512,1024]{1,0:T(8,128)}, u32[]{:S(2)}) copy-start(f32[512,1024]{1,0:T(8,128)} %copy-done.9) | copy-start | bytes 6291460
  1103.4 202.4 %all-to-all-start = ((bf16[8,128,1024]{1,2,0:T(8,128)(2,1)}), bf16[8,128,1024]{1,2,0:T(8,128)(2,1)}, u32[]{:S(2)}, u32[]{:S(2)}) async-start(bf16[8,128,1024]{1,2,0:T(8,128)(2,1)} %copy.73), calls=%async_computation.4 | async-start | bytes 4194304 | tf_op jit(solution)/shard_map/all_to_all | solution.py:20
  (22 other events, 60.9 us)
Sparse Core Ops, SparseCore 0:
  10.7 48.1 all-gather.10
  61.0 33.1 all-gather.8
  301.2 42.1 reduce-scatter.12
  345.6 49.2 all-gather.14
  397.0 32.9 all-gather.12
  432.2 49.2 all-gather.16
  483.1 32.9 all-gather.18
  539.0 44.4 reduce-scatter.16
  586.0 44.4 reduce-scatter.14
  637.7 34.4 all-gather.20
  1028.0 44.5 reduce-scatter.18
  1074.7 140.0 reduce-scatter.26
  1218.8 84.8 reduce-scatter.22
  1305.9 133.5 reduce-scatter.24
  1444.0 83.7 reduce-scatter.20
where the time goes:
time: 1540 us; the launch traced here: 1530 us
  waiting for transfers between devices  702 us (46%)
  local copies, waits for them, and re-layouts  291 us (19%)
  matrix products  275 us (18%)
  blocking collectives  119 us (8%)
  other arithmetic  106 us (7%)
  loops' own time  18.6 us (1%)
    unnamed x17, waiting for transfers between devices  232 us
    broadcast_in_dim x16, local copies, waits for them, and re-layouts, tile_scores(): scores = jnp.where(keep_mask, scores, NEGATIVE)  226 us
    reduce_scatter x4, waiting for transfers between devices, sum_rows(): lax.psum_scatter(partial_rows.astype(jnp.bfloat16), 'tensor', scatter_dim...  146 us
    all_gather x4, waiting for transfers between devices, gather_rows(): return lax.all_gather(local_rows, 'tensor', axis=0, tiled=True)  104 us
    reduce_scatter x1, waiting for transfers between devices, per_device(): lax.psum_scatter(grad_down, 'dp', scatter_dimension=0, tiled=True)  87.6 us
    reduce_scatter x1, waiting for transfers between devices, per_device(): lax.psum_scatter(grad_up, 'dp', scatter_dimension=0, tiled=True)  86.9 us
    dot_general x8, matrix products, tile_scores(): jnp.einsum('qhd,khd->hqk', query_tile, key_rows, preferred_element_type=j...  73.4 us
    convert_element_type x4, other arithmetic, one_tile(): (probabilities * (grad_probs - row_inner)).astype(jnp.bfloat16)  45.9 us
  transfers between devices with their start and end apart: 16, of which 13 were waited for; matrix products, arithmetic and copies ran while one was open for 6% of the time, Pallas kernels for 0%

commit v1 on v0

--- a/solution.py
+++ b/solution.py
@@ -8,6 +8,27 @@
 BLOCK = 64
 EPS = 1e-05
 NEGATIVE = -1e30
+
+
+def gather_around(array, axis, dim):
+    count, place, extent = (lax.axis_size(axis), lax.axis_index(axis), array.shape[dim])
+    upward = [(i, (i + 1) % count) for i in range(count)]
+    behind = [(i, (i - 1) % count) for i in range(count)]
+    whole = jnp.zeros((*array.shape[:dim], count * extent, *array.shape[dim + 1 :]), array.dtype)
+    whole = lax.dynamic_update_slice_in_dim(whole, array, place * extent, axis=dim)
+    from_left = from_right = array
+    middle = count // 2
+    for step in range(1, middle + 1):
+        from_left = lax.ppermute(from_left, axis, upward)
+        whole = lax.dynamic_update_slice_in_dim(
+            whole, from_left, (place - step) % count * extent, axis=dim
+        )
+        if step < count - middle:
+            from_right = lax.ppermute(from_right, axis, behind)
+            whole = lax.dynamic_update_slice_in_dim(
+                whole, from_right, (place + step) % count * extent, axis=dim
+            )
+    return whole
 
 
 def in_blocks(value, dim, count):
@@ -67,7 +88,7 @@
 def attention_weights(qkv_weight, out_weight):
     return (
         lax.all_gather(qkv_weight, "dp", axis=0, tiled=True),
-        lax.all_gather(out_weight, "dp", axis=0, tiled=True),
+        gather_around(out_weight, "dp", 0),
     )
 
 

time: 1540 us -> 1540 us (level)
  blocking collectives: 119 us -> 84.7 us
  waiting for transfers between devices: 702 us -> 721 us
    all_gather x1 -> x0, blocking collectives: 33.9 us -> none  [attention_weights(): lax.all_gather(out_weight, 'dp', axis=0, tiled=True)]
  transfers between devices with their start and end apart: 16 -> 23, of which waited for: 13 -> 18; matrix products, arithmetic and copies ran while one was open for 6% -> 7% of each run, Pallas kernels for 0% -> 0%
where the time goes in v1:
time: 1540 us
  waiting for transfers between devices  721 us (47%)
  local copies, waits for them, and re-layouts  297 us (19%)
  matrix products  275 us (18%)
  other arithmetic  106 us (7%)
  blocking collectives  84.7 us (6%)
  loops' own time  19.1 us (1%)
  starting transfers between devices  17.2 us (1%)
    unnamed x17, waiting for transfers between devices  233 us
    broadcast_in_dim x16, local copies, waits for them, and re-layouts, tile_scores(): scores = jnp.where(keep_mask, scores, NEGATIVE)  225 us
    reduce_scatter x4, waiting for transfers between devices, sum_rows(): lax.psum_scatter(partial_rows.astype(jnp.bfloat16), 'tensor', scatter_dim...  148 us
    all_gather x4, waiting for transfers between devices, gather_rows(): return lax.all_gather(local_rows, 'tensor', axis=0, tiled=True)  108 us
    reduce_scatter x1, waiting for transfers between devices, per_device(): lax.psum_scatter(grad_down, 'dp', scatter_dimension=0, tiled=True)  87.2 us
    reduce_scatter x1, waiting for transfers between devices, per_device(): lax.psum_scatter(grad_up, 'dp', scatter_dimension=0, tiled=True)  87.1 us
    dot_general x8, matrix products, tile_scores(): jnp.einsum('qhd,khd->hqk', query_tile, key_rows, preferred_element_type=j...  72.9 us
    convert_element_type x4, other arithmetic, one_tile(): (probabilities * (grad_probs - row_inner)).astype(jnp.bfloat16)  45.9 us
  transfers between devices with their start and end apart: 23, of which 18 were waited for; matrix products, arithmetic and copies ran while one was open for 7% of the time, Pallas kernels for 0%

profile of v1, /device:TPU:0, one launch (start us, length us, event | category | flops | bytes accessed | tf_op | source)
XLA Modules:
  0.0 1536.0 jit_solution(14438605661853323666)
XLA Ops:
  9.1 44.2 %all-gather = f32[32,32,8]{1,2,0:T(8,128)S(1)} all-gather(f32[1,32,8]{1,2,0:T(8,128)} %bitcast.196), channel_id=1, replica_groups=mesh['dp'=8,'tensor'=4] {'dp','tensor'}, dimensions={0}, use_global_device_ids=true | all-gather | bytes 33792 | tf_op jit(solution)/shard_map/all_gather | solution.py:236
  102.8 192.3 %while.28 = (s32[]{:T(128)}, bf16[4,512,256]{2,1,0:T(8,128)(2,1)}, f32[4,4,512]{2,1,0:T(4,128)S(1)}, s32[4]{0:T(128)S(1)}, pred[4,32,32]{2,1,0:T(8,128)(4,1)S(1)...) while((s32[]{:T(128)}, bf16[4,512,256]{2,1,0:T(8,128)(2,1)}, ...), condition=%wide.region_6.7_spmd.clone, body=%wide.region_3.6_spmd.clone.sunk | while | flops 1124272128 | bytes 96148904 | solution.py:162
  111.0 22.8 %broadcast_in_dim.121 = pred[4,512,2048]{2,1,0:T(32,128)(4,1)} reshape(pred[4,8,64,32,64]{4,3,2,1,0:T(32,128)(4,1)} %broadcast_in_dim.120) | data formatting | bytes 8388608 | tf_op jit(solution)/shard_map/while/body/eval_jaxpr/jit(_where)/broadcast_in_dim | solution.py:130
  144.2 5.8 fusion.136
  159.1 22.8 %broadcast_in_dim.121 = pred[4,512,2048]{2,1,0:T(32,128)(4,1)} reshape(pred[4,8,64,32,64]{4,3,2,1,0:T(32,128)(4,1)} %broadcast_in_dim.120) | data formatting | bytes 8388608 | tf_op jit(solution)/shard_map/while/body/eval_jaxpr/jit(_where)/broadcast_in_dim | solution.py:130
  192.2 5.8 fusion.136
  207.1 22.8 %broadcast_in_dim.121 = pred[4,512,2048]{2,1,0:T(32,128)(4,1)} reshape(pred[4,8,64,32,64]{4,3,2,1,0:T(32,128)(4,1)} %broadcast_in_dim.120) | data formatting | bytes 8388608 | tf_op jit(solution)/shard_map/while/body/eval_jaxpr/jit(_where)/broadcast_in_dim | solution.py:130
  240.3 5.8 fusion.136
  255.2 22.8 %broadcast_in_dim.121 = pred[4,512,2048]{2,1,0:T(32,128)(4,1)} reshape(pred[4,8,64,32,64]{4,3,2,1,0:T(32,128)(4,1)} %broadcast_in_dim.120) | data formatting | bytes 8388608 | tf_op jit(solution)/shard_map/while/body/eval_jaxpr/jit(_where)/broadcast_in_dim | solution.py:130
  288.4 5.8 fusion.136
  300.5 43.9 %reduce-scatter.13.cloned.1.call-done = bf16[512,1024]{1,0:T(8,128)(2,1)} async-done(((bf16[2048,1024]{1,0:T(8,128)(2,1)}), bf16[512,1024]{1,0:T(8,128)(2,1)}) %reduce-scatter.13.cloned.1.call-update) | async-done | bytes 1048592 | tf_op jit(solution)/shard_map/reduce_scatter | solution.py:83
  351.0 40.5 %all_gather.37 = f32[1,4096]{1,0:T(1,128)S(1)} all-gather(f32[1,128]{1,0:T(1,128)S(1)} %copy-done.34), channel_id=1, replica_groups=mesh['dp'=8,'tensor'=4] {'dp','tensor'}, dimensions={1}, use_global_device_ids=true | all-gather | bytes 16896 | tf_op jit(solution)/shard_map/all_gather | solution.py:237
  395.9 35.1 %all-gather.13.cloned.1.call-done = bf16[2048,1024]{1,0:T(8,128)(2,1)} async-done(((bf16[512,1024]{1,0:T(8,128)(2,1)}), bf16[2048,1024]{1,0:T(8,128)(2,1)}) %all-gather.13.cloned.1.call-update) | async-done | bytes 4194320 | tf_op jit(solution)/shard_map/all_gather | solution.py:79
  431.0 10.6 fusion.87
  441.6 40.9 %all-gather.17.cloned.1.call-done = bf16[1024,1024]{1,0:T(8,128)(2,1)} async-done(((bf16[128,1024]{1,0:T(8,128)(2,1)}), bf16[1024,1024]{1,0:T(8,128)(2,1)}) %all-gather.17.cloned.1.call-update) | async-done | bytes 2097168 | tf_op jit(solution)/shard_map/all_gather | solution.py:98
  482.5 34.6 %all-gather.19.cloned.1.call-done = bf16[2048,1024]{1,0:T(8,128)(2,1)} async-done(((bf16[512,1024]{1,0:T(8,128)(2,1)}), bf16[2048,1024]{1,0:T(8,128)(2,1)}) %all-gather.19.cloned.1.call-update) | async-done | bytes 4194320 | tf_op jit(solution)/shard_map/all_gather | solution.py:79
  517.2 14.3 convert_reduce_fusion
  533.5 6.3 convolution_convert_fusion.1
  540.1 11.8 convolution_convert_fusion.2
  552.0 32.6 %reduce-scatter.17.cloned.1.call-done = bf16[512,1024]{1,0:T(8,128)(2,1)} async-done(((bf16[2048,1024]{1,0:T(8,128)(2,1)}), bf16[512,1024]{1,0:T(8,128)(2,1)}) %reduce-scatter.17.cloned.1.call-update) | async-done | bytes 1048592 | tf_op jit(solution)/shard_map/reduce_scatter | solution.py:83
  587.9 43.7 %reduce-scatter.15.cloned.1.call-done = bf16[512,1024]{1,0:T(8,128)(2,1)} async-done(((bf16[2048,1024]{1,0:T(8,128)(2,1)}), bf16[512,1024]{1,0:T(8,128)(2,1)}) %reduce-scatter.15.cloned.1.call-update) | async-done | bytes 1048592 | tf_op jit(solution)/shard_map/reduce_scatter | solution.py:83
  638.7 34.6 %all-gather.21.cloned.1.call-done = bf16[2048,1024]{1,0:T(8,128)(2,1)} async-done(((bf16[512,1024]{1,0:T(8,128)(2,1)}), bf16[2048,1024]{1,0:T(8,128)(2,1)}) %all-gather.21.cloned.1.call-update) | async-done | bytes 4194320 | tf_op jit(solution)/shard_map/all_gather | solution.py:79
  677.9 328.6 %while.29 = (s32[]{:T(128)}, f32[2048,4,64]{0,2,1:T(8,128)}, f32[2048,4,64]{0,2,1:T(8,128)}, bf16[4,512,4,64]{1,3,2,0:T(8,128)(2,1)}, s32[4]{0:T(128)S(1)}, /*in...) while((s32[]{:T(128)}, f32[2048,4,64]{0,2,1:T(8,128)}, ...), condition=%wide.region_16.17_spmd.clone, body=%wide.region_14.16_spmd.clone.sunk | while | flops 2725054464 | bytes 256294480 | solution.py:211
  688.4 22.8 %broadcast_in_dim.123 = pred[4,512,2048]{2,1,0:T(32,128)(4,1)} reshape(pred[4,8,64,32,64]{4,3,2,1,0:T(32,128)(4,1)} %broadcast_in_dim.122) | data formatting | bytes 8388608 | tf_op jit(solution)/shard_map/while/body/eval_jaxpr/jit(_where)/broadcast_in_dim | solution.py:130
  711.2 9.2 fusion.146
  720.4 12.6 multiply_reduce_fusion.3
  733.0 11.5 multiply_convert_fusion.5
  769.9 22.8 %broadcast_in_dim.123 = pred[4,512,2048]{2,1,0:T(32,128)(4,1)} reshape(pred[4,8,64,32,64]{4,3,2,1,0:T(32,128)(4,1)} %broadcast_in_dim.122) | data formatting | bytes 8388608 | tf_op jit(solution)/shard_map/while/body/eval_jaxpr/jit(_where)/broadcast_in_dim | solution.py:130
  792.7 9.2 fusion.146
  801.9 12.6 multiply_reduce_fusion.3
  814.5 11.5 multiply_convert_fusion.5
  852.1 22.8 %broadcast_in_dim.123 = pred[4,512,2048]{2,1,0:T(32,128)(4,1)} reshape(pred[4,8,64,32,64]{4,3,2,1,0:T(32,128)(4,1)} %broadcast_in_dim.122) | data formatting | bytes 8388608 | tf_op jit(solution)/shard_map/while/body/eval_jaxpr/jit(_where)/broadcast_in_dim | solution.py:130
  874.9 9.2 fusion.146
  884.1 12.6 multiply_reduce_fusion.3
  896.7 11.5 multiply_convert_fusion.5
  934.3 22.8 %broadcast_in_dim.123 = pred[4,512,2048]{2,1,0:T(32,128)(4,1)} reshape(pred[4,8,64,32,64]{4,3,2,1,0:T(32,128)(4,1)} %broadcast_in_dim.122) | data formatting | bytes 8388608 | tf_op jit(solution)/shard_map/while/body/eval_jaxpr/jit(_where)/broadcast_in_dim | solution.py:130
  957.1 9.2 fusion.146
  966.3 12.6 multiply_reduce_fusion.3
  978.9 11.5 multiply_convert_fusion.5
  1021.2 7.8 bitcast_convert_fusion
  1031.8 13.3 convolution_bitcast_fusion
  1045.9 27.8 %reduce-scatter.19.cloned.1.call-done = bf16[512,1024]{1,0:T(8,128)(2,1)} async-done(((bf16[2048,1024]{1,0:T(8,128)(2,1)}), bf16[512,1024]{1,0:T(8,128)(2,1)}) %reduce-scatter.19.cloned.1.call-update) | async-done | bytes 1048592 | tf_op jit(solution)/shard_map/reduce_scatter | solution.py:83
  1077.7 10.0 fusion.88
  1092.7 7.8 fusion.73
  1110.2 106.1 %reduce-scatter.27.cloned.1.call-done = f32[128,1]{1,0:T(8,128)} async-done(((f32[4096,1]{1,0:T(8,128)}), f32[128,1]{1,0:T(8,128)}) %reduce-scatter.27.cloned.1.call-update) | async-done | bytes 528
  1217.8 87.2 %reduce-scatter.23.cloned.1.call-done = f32[128,1024]{0,1:T(8,128)} async-done(((f32[1024,1024]{0,1:T(8,128)}), f32[128,1024]{0,1:T(8,128)}) %reduce-scatter.23.cloned.1.call-update) | async-done | bytes 524304 | tf_op jit(solution)/shard_map/reduce_scatter | solution.py:294
  1315.9 124.9 %reduce-scatter.25.cloned.1.call-done = f32[32,8]{1,0:T(8,128)} async-done(((f32[1024,8]{1,0:T(8,128)}), f32[32,8]{1,0:T(8,128)}) %reduce-scatter.25.cloned.1.call-update) | async-done | bytes 1040
  1442.2 87.1 %reduce-scatter.21.cloned.1.call-done = f32[128,1024]{1,0:T(8,128)} async-done(((f32[1024,1024]{1,0:T(8,128)}), f32[128,1024]{1,0:T(8,128)}) %reduce-scatter.21.cloned.1.call-update) | async-done | bytes 524304 | tf_op jit(solution)/shard_map/reduce_scatter | solution.py:293
  (321 shorter events, 297.8 us)
Async XLA Ops:
  7.2 53.3 %copy-start.16 = (bf16[128,256]{1,0:T(8,128)(2,1)S(1)}, bf16[128,256]{1,0:T(8,128)(2,1)}, u32[]{:S(2)}) copy-start(bf16[128,256]{1,0:T(8,128)(2,1)} %param.21) | copy-start | bytes 196612
  7.2 56.1 %copy-start.30 = (s32[1,4,32,3]{2,1,3,0:T(4,128)S(1)}, s32[1,4,32,3]{2,1,3,0:T(4,128)}, u32[]{:S(2)}) copy-start(s32[1,4,32,3]{2,1,3,0:T(4,128)} %param.19) | copy-start | bytes 4612
  7.2 56.2 %copy-start.29 = (s32[1,32]{1,0:T(1,128)S(1)}, s32[1,32]{1,0:T(1,128)}, u32[]{:S(2)}) copy-start(s32[1,32]{1,0:T(1,128)} %param.18) | copy-start | bytes 388
  7.2 83.8 %all-gather.11.cloned.1.call-start = ((), (), s32[]{:S(2)}) async-start(), calls=%async_computation.10 | async-start | bytes 1769472 | tf_op jit(solution)/shard_map/all_gather | solution.py:90
  9.0 86.0 %all-gather.9.cloned.1.call-start = ((), (), s32[]{:S(2)}) async-start(), calls=%async_computation.9 | async-start | bytes 5242880 | tf_op jit(solution)/shard_map/all_gather | solution.py:79
  60.4 283.9 %reduce-scatter.13.cloned.1.call-start = ((), (), s32[]{:S(2)}) async-start(), calls=%async_computation.11 | async-start | bytes 5242880 | tf_op jit(solution)/shard_map/reduce_scatter | solution.py:83
  60.5 5.7 collective-permute-start.1
  60.6 8.4 collective-permute-start
  66.2 4.7 collective-permute-start.3
  69.0 7.1 collective-permute-start.2
  70.9 13.2 collective-permute-start.5
  76.0 7.0 collective-permute-start.4
  83.0 7.4 collective-permute-start.6
  299.7 44.7 %copy-start.3 = (bf16[512,1024]{1,0:T(8,128)(2,1)S(1)}, bf16[512,1024]{1,0:T(8,128)(2,1)}, u32[]{:S(2)}) copy-start(bf16[512,1024]{1,0:T(8,128)(2,1)} %param.15) | copy-start | bytes 3145732
  299.7 44.7 %copy-start.14 = (f32[1,1024]{1,0:T(1,128)S(1)}, f32[1,1024]{1,0:T(1,128)}, u32[]{:S(2)}) copy-start(f32[1,1024]{1,0:T(1,128)} %get-tuple-element.298) | copy-start | bytes 12292
  299.7 48.3 %copy-start.15 = (f32[1,1024]{1,0:T(1,128)S(1)}, f32[1,1024]{1,0:T(1,128)}, u32[]{:S(2)}) copy-start(f32[1,1024]{1,0:T(1,128)} %get-tuple-element.297) | copy-start | bytes 12292
  299.7 48.3 %copy-start.24 = (f32[1,1024]{1,0:T(1,128)S(1)}, f32[1,1024]{1,0:T(1,128)}, u32[]{:S(2)}) copy-start(f32[1,1024]{1,0:T(1,128)} %get-tuple-element.296) | copy-start | bytes 12292
  299.7 96.2 %all-gather.15.cloned.1.call-start = ((), (), s32[]{:S(2)}) async-start(), calls=%async_computation.13 | async-start | bytes 2359296 | tf_op jit(solution)/shard_map/all_gather | solution.py:97
  300.3 130.7 %all-gather.13.cloned.1.call-start = ((), (), s32[]{:S(2)}) async-start(), calls=%async_computation.12 | async-start | bytes 5242880 | tf_op jit(solution)/shard_map/all_gather | solution.py:79
  349.6 133.0 %all-gather.17.cloned.1.call-start = ((), (), s32[]{:S(2)}) async-start(), calls=%async_computation.14 | async-start | bytes 2359296 | tf_op jit(solution)/shard_map/all_gather | solution.py:98
  350.1 167.0 %all-gather.19.cloned.1.call-start = ((), (), s32[]{:S(2)}) async-start(), calls=%async_computation.16 | async-start | bytes 5242880 | tf_op jit(solution)/shard_map/all_gather | solution.py:79
  350.9 233.7 %reduce-scatter.17.cloned.1.call-start = ((), (), s32[]{:S(2)}) async-start(), calls=%async_computation.17 | async-start | bytes 5242880 | tf_op jit(solution)/shard_map/reduce_scatter | solution.py:83
  391.4 148.7 %copy-start.31 = (f32[1,1024]{1,0:T(1,128)}, f32[1,1024]{1,0:T(1,128)S(1)}, u32[]{:S(2)}) copy-start(f32[1,1024]{1,0:T(1,128)S(1)} %constant_dynamic-slice_fusion.2) | copy-start | bytes 12292
  517.2 16.3 %copy-start.35 = (bf16[1024,1024]{1,0:T(8,128)(2,1)S(1)}, bf16[1024,1024]{1,0:T(8,128)(2,1)}, u32[]{:S(2)}) copy-start(bf16[1024,1024]{1,0:T(8,128)(2,1)} %all-gather.15.cloned.1.call-done) | copy-start | bytes 6291460
  539.9 91.7 %reduce-scatter.15.cloned.1.call-start = ((), (), s32[]{:S(2)}) async-start(), calls=%async_computation.15 | async-start | bytes 5242880 | tf_op jit(solution)/shard_map/reduce_scatter | solution.py:83
  551.9 79.7 %copy-start.23 = (f32[1,1024]{1,0:T(1,128)S(1)}, f32[1,1024]{1,0:T(1,128)}, u32[]{:S(2)}) copy-start(f32[1,1024]{1,0:T(1,128)} %get-tuple-element.295) | copy-start | bytes 12292
  551.9 121.4 %all-gather.21.cloned.1.call-start = ((), (), s32[]{:S(2)}) async-start(), calls=%async_computation.18 | async-start | bytes 5242880 | tf_op jit(solution)/shard_map/all_gather | solution.py:79
  638.6 435.1 %reduce-scatter.19.cloned.1.call-start = ((), (), s32[]{:S(2)}) async-start(), calls=%async_computation.19 | async-start | bytes 5242880 | tf_op jit(solution)/shard_map/reduce_scatter | solution.py:83
  733.0 15.4 %copy-start = (f32[4,512,2048]{2,1,0:T(8,128)S(1)}, f32[4,512,2048]{2,1,0:T(8,128)}, u32[]{:S(2)}) copy-start(f32[4,512,2048]{2,1,0:T(8,128)} %get-tuple-element.455) | copy-start | bytes 50331652 | tf_op jit(solution)/shard_map/while
  814.5 15.4 %copy-start = (f32[4,512,2048]{2,1,0:T(8,128)S(1)}, f32[4,512,2048]{2,1,0:T(8,128)}, u32[]{:S(2)}) copy-start(f32[4,512,2048]{2,1,0:T(8,128)} %get-tuple-element.455) | copy-start | bytes 50331652 | tf_op jit(solution)/shard_map/while
  896.7 15.4 %copy-start = (f32[4,512,2048]{2,1,0:T(8,128)S(1)}, f32[4,512,2048]{2,1,0:T(8,128)}, u32[]{:S(2)}) copy-start(f32[4,512,2048]{2,1,0:T(8,128)} %get-tuple-element.455) | copy-start | bytes 50331652 | tf_op jit(solution)/shard_map/while
  957.1 9.2 copy-start.2
  978.9 15.4 %copy-start = (f32[4,512,2048]{2,1,0:T(8,128)S(1)}, f32[4,512,2048]{2,1,0:T(8,128)}, u32[]{:S(2)}) copy-start(f32[4,512,2048]{2,1,0:T(8,128)} %get-tuple-element.455) | copy-start | bytes 50331652 | tf_op jit(solution)/shard_map/while
  1009.3 9.3 copy-start.7
  1029.0 187.3 %reduce-scatter.27.cloned.1.call-start = ((), (), s32[]{:S(2)}) async-start(), calls=%async_computation.23 | async-start | bytes 2162688
  1031.7 273.3 %reduce-scatter.23.cloned.1.call-start = ((), (), s32[]{:S(2)}) async-start(), calls=%async_computation.21 | async-start | bytes 4718592 | tf_op jit(solution)/shard_map/reduce_scatter | solution.py:294
  1045.1 28.6 %copy-start.4 = (bf16[512,1024]{1,0:T(8,128)(2,1)S(1)}, bf16[512,1024]{1,0:T(8,128)(2,1)}, u32[]{:S(2)}) copy-start(bf16[512,1024]{1,0:T(8,128)(2,1)} %param.15) | copy-start | bytes 3145732
  1045.1 28.6 %copy-start.18 = (f32[1,1024]{1,0:T(1,128)S(1)}, f32[1,1024]{1,0:T(1,128)}, u32[]{:S(2)}) copy-start(f32[1,1024]{1,0:T(1,128)} %copy-done.17) | copy-start | bytes 12292
  1045.1 28.6 %copy-start.20 = (f32[512]{0:T(512)S(1)}, f32[512]{0:T(512)}, u32[]{:S(2)}) copy-start(f32[512]{0:T(512)} %copy-done.19) | copy-start | bytes 6148
  1045.1 28.6 %copy-start.22 = (f32[512]{0:T(512)S(1)}, f32[512]{0:T(512)}, u32[]{:S(2)}) copy-start(f32[512]{0:T(512)} %copy-done.21) | copy-start | bytes 6148
  1045.1 31.4 %copy-start.25 = (f32[1024]{0:T(1024)S(1)}, f32[1024]{0:T(1024)}, u32[]{:S(2)}) copy-start(f32[1024]{0:T(1024)} %get-tuple-element.227) | copy-start | bytes 12292
  1045.1 31.4 %copy-start.26 = (f32[1024]{0:T(1024)S(1)}, f32[1024]{0:T(1024)}, u32[]{:S(2)}) copy-start(f32[1024]{0:T(1024)} %get-tuple-element.233) | copy-start | bytes 12292
  1045.2 31.4 %copy-start.27 = (f32[1024]{0:T(1024)S(1)}, f32[1024]{0:T(1024)}, u32[]{:S(2)}) copy-start(f32[1024]{0:T(1024)} %get-tuple-element.285) | copy-start | bytes 12292
  1045.2 31.4 %copy-start.28 = (f32[1024]{0:T(1024)S(1)}, f32[1024]{0:T(1024)}, u32[]{:S(2)}) copy-start(f32[1024]{0:T(1024)} %get-tuple-element.294) | copy-start | bytes 12292
  1045.2 395.6 %reduce-scatter.25.cloned.1.call-start = ((), (), s32[]{:S(2)}) async-start(), calls=%async_computation.22 | async-start | bytes 540672
  1077.6 451.7 %reduce-scatter.21.cloned.1.call-start = ((), (), s32[]{:S(2)}) async-start(), calls=%async_computation.20 | async-start | bytes 4718592 | tf_op jit(solution)/shard_map/reduce_scatter | solution.py:293
  1104.6 208.4 %copy-start.10 = (f32[512,1024]{1,0:T(8,128)S(1)}, f32[512,1024]{1,0:T(8,128)}, u32[]{:S(2)}) copy-start(f32[512,1024]{1,0:T(8,128)} %copy-done.9) | copy-start | bytes 6291460
  1104.6 202.5 %all-to-all-start = ((bf16[8,128,1024]{1,2,0:T(8,128)(2,1)}), bf16[8,128,1024]{1,2,0:T(8,128)(2,1)}, u32[]{:S(2)}, u32[]{:S(2)}) async-start(bf16[8,128,1024]{1,2,0:T(8,128)(2,1)} %copy.73), calls=%async_computation.4 | async-start | bytes 4194304 | tf_op jit(solution)/shard_map/all_to_all | solution.py:41
  (27 other events, 102.1 us)
Sparse Core Ops, SparseCore 0:
  10.7 49.4 all-gather.10
  62.3 32.6 all-gather.8
  299.8 44.5 reduce-scatter.12
  346.6 49.2 all-gather.14
  398.0 32.9 all-gather.12
  433.2 49.2 all-gather.16
  484.2 32.9 all-gather.18
  540.0 44.5 reduce-scatter.16
  587.1 44.4 reduce-scatter.14
  638.8 34.4 all-gather.20
  1029.2 44.5 reduce-scatter.18
  1075.8 140.5 reduce-scatter.26
  1220.4 84.5 reduce-scatter.22
  1307.1 133.6 reduce-scatter.24
  1445.3 83.9 reduce-scatter.20
